TPU v7x, 32 devices: a whole 2x2x4 slice. The times are simulated.
32 devices in a mesh: gx: 8 (over z, y), gy: 4 (over x, core).
Axes of the slice: x: 2, y: 2, z: 4, core: 2. Of those that a mesh axis runs over, the one named last changes fastest.
Arguments:
- psi: float32 [2, 256, 16, 1024], P(None, 'gx', None, 'gy'), may hold values from -6 to 6
- potential: float32 [256, 16, 1024], P('gx', None, 'gy'), may hold values from 0 to 4
Outputs:
- psi_half: float32 [2, 256, 16, 1024], P(None, 'gx', None, 'gy')
All inputs are finite; a program needn't handle non-finite values.
Results may differ from a plain program's by a relative error of at most 0.00005.
Values sent between devices are 32-bit elements; how exact they have to be, the bound alone decides.
A program may use at most 64 MiB of HBM per device.

v0:
```python
import jax
import jax.numpy as jnp
import numpy as np
from jax import lax
from jax.sharding import PartitionSpec as P

RYZ = 2


def with_halo(value, sides, width):
    for axis, dim in sides:
        peers, length = (lax.axis_size(axis), value.shape[dim])
        up = [(i, (i + 1) % peers) for i in range(peers - 1)]
        down = [(j, i) for i, j in up]
        last = lax.slice_in_dim(value, length - width, length, axis=dim)
        first = lax.slice_in_dim(value, 0, width, axis=dim)
        before = lax.ppermute(last, axis, up)
        after = lax.ppermute(first, axis, down)
        value = jnp.concatenate([before, value, after], axis=dim)
    return value


def cmul(left, right):
    return jnp.stack(
        [left[0] * right[0] - left[1] * right[1], left[0] * right[1] + left[1] * right[0]]
    )


def cinv(value):
    denom = value[0] * value[0] + value[1] * value[1]
    return jnp.stack([value[0] / denom, -value[1] / denom])


def local_inverse(cells):
    coef = 256.0 * cells * cells
    identity = np.eye(cells)
    cp_re_list = []
    cp_im_list = []
    dp_re_list = []
    dp_im_list = []
    cp_re = 0.0
    cp_im = 0.0
    dp_re = np.zeros(cells)
    dp_im = np.zeros(cells)
    for index in range(cells):
        piv_re = 1.0 - coef * cp_im
        piv_im = 2.0 * coef + coef * cp_re
        denom = piv_re * piv_re + piv_im * piv_im
        cp_re = -coef * piv_im / denom
        cp_im = -coef * piv_re / denom
        num_re = identity[index] - coef * dp_im
        num_im = coef * dp_re
        dp_re = (num_re * piv_re + num_im * piv_im) / denom
        dp_im = (num_im * piv_re - num_re * piv_im) / denom
        cp_re_list.append(cp_re)
        cp_im_list.append(cp_im)
        dp_re_list.append(dp_re)
        dp_im_list.append(dp_im)
    inv_re = np.zeros((cells, cells))
    inv_im = np.zeros((cells, cells))
    later_re = np.zeros(cells)
    later_im = np.zeros(cells)
    for index in range(cells - 1, -1, -1):
        next_re = dp_re_list[index] - (cp_re_list[index] * later_re - cp_im_list[index] * later_im)
        next_im = dp_im_list[index] - (cp_re_list[index] * later_im + cp_im_list[index] * later_re)
        later_re, later_im = (next_re, next_im)
        inv_re[index] = later_re
        inv_im[index] = later_im
    return (inv_re, inv_im, coef)


def shards(psi, potential):
    cells = psi.shape[1]
    count = lax.axis_size("gx")
    place = lax.axis_index("gx")
    inv_re, inv_im, coef = local_inverse(cells)
    upper_half = np.concatenate([inv_re, -inv_im], axis=1)
    lower_half = np.concatenate([inv_im, inv_re], axis=1)
    big = np.concatenate([upper_half, lower_half], axis=0).astype(np.float32)
    g_vec = jnp.asarray(np.stack([-coef * inv_im[:, 0], coef * inv_re[:, 0]]).astype(np.float32))
    h_vec = jnp.asarray(
        np.stack([-coef * inv_im[:, cells - 1], coef * inv_re[:, cells - 1]]).astype(np.float32)
    )
    s_val = g_vec[:, 0]
    t_val = g_vec[:, cells - 1]
    real_part, imag_part = (psi[0], psi[1])
    theta = 0.5 * (potential + real_part * real_part + imag_part * imag_part)
    cosine, sine = (jnp.cos(theta), jnp.sin(theta))
    turned = jnp.stack(
        [real_part * cosine + imag_part * sine, imag_part * cosine - real_part * sine]
    )
    padded = with_halo(turned, (("gy", 3),), 1)
    lap_y = padded[:, :, :, 2:] + padded[:, :, :, :-2] - 2.0 * turned
    z_padded = jnp.pad(turned, ((0, 0), (0, 0), (1, 1), (0, 0)))
    lap_z = z_padded[:, :, 2:] + z_padded[:, :, :-2] - 2.0 * turned
    side = RYZ * (lap_y + lap_z)
    rhs = jnp.stack([2.0 * turned[0] - side[1], 2.0 * turned[1] + side[0]])
    planes = rhs.shape[2]
    lines = rhs.shape[3]
    flat = rhs.reshape(2 * cells, planes * lines)
    local = jnp.dot(jnp.asarray(big), flat, precision=lax.Precision.HIGHEST).reshape(
        2, cells, planes, lines
    )
    first_val = local[:, 0]
    last_val = local[:, cells - 1]

    def advance(alpha, unused):
        q_val = cinv(
            jnp.stack(
                [
                    1.0 - (s_val[0] * alpha[0] - s_val[1] * alpha[1]),
                    -(s_val[0] * alpha[1] + s_val[1] * alpha[0]),
                ]
            )
        )
        aq_val = cmul(alpha, q_val)
        c_val = cmul(t_val, jnp.stack([1.0, 0.0]) + cmul(aq_val, s_val))
        mu_val = cmul(q_val, t_val)
        new_alpha = s_val + cmul(cmul(t_val, t_val), aq_val)
        return (new_alpha, (alpha, q_val, c_val, mu_val))

    unused, tables = lax.scan(advance, jnp.zeros((2,), jnp.float32), None, length=count)
    alphas, q_vals, c_vals, mu_vals = tables
    alpha_here = lax.dynamic_index_in_dim(alphas, place, 0, keepdims=False)
    q_here = lax.dynamic_index_in_dim(q_vals, place, 0, keepdims=False)
    mu_here = lax.dynamic_index_in_dim(mu_vals, place, 0, keepdims=False)
    fwd_term = last_val + cmul(cmul(t_val, cmul(alpha_here, q_here)), first_val)
    positions = jnp.arange(count, dtype=jnp.int32)

    def fwd_row(row, item):
        factor, index = item
        onehot = jnp.stack(
            [(positions == index).astype(jnp.float32), jnp.zeros((count,), jnp.float32)]
        )
        return (cmul(factor, row) + onehot, row)

    unused, fwd_rows = lax.scan(fwd_row, jnp.zeros((2, count), jnp.float32), (c_vals, positions))
    fwd_weights = lax.dynamic_index_in_dim(fwd_rows, place, 0, keepdims=False)
    piece = lax.all_gather(fwd_term[None], "gx", axis=0, tiled=True)
    weights = lax.slice_in_dim(fwd_weights, 0, piece.shape[0], axis=1)
    part_re = jnp.einsum(
        "k,kzy->zy", weights[0], piece[:, 0], precision=lax.Precision.HIGHEST
    ) - jnp.einsum("k,kzy->zy", weights[1], piece[:, 1], precision=lax.Precision.HIGHEST)
    part_im = jnp.einsum(
        "k,kzy->zy", weights[0], piece[:, 1], precision=lax.Precision.HIGHEST
    ) + jnp.einsum("k,kzy->zy", weights[1], piece[:, 0], precision=lax.Precision.HIGHEST)
    beta_prev = jnp.zeros_like(fwd_term) + jnp.stack([part_re, part_im])
    nu_here = cmul(q_here, first_val + cmul(s_val, beta_prev))

    def back_row(row, item):
        factor, index = item
        onehot = jnp.stack(
            [(positions == index).astype(jnp.float32), jnp.zeros((count,), jnp.float32)]
        )
        return (cmul(factor, row) + onehot, row)

    unused, back_rows = lax.scan(
        back_row, jnp.zeros((2, count), jnp.float32), (mu_vals, positions), reverse=True
    )
    back_weights = lax.dynamic_index_in_dim(back_rows, place, 0, keepdims=False)
    piece = lax.all_gather(nu_here[None], "gx", axis=0, tiled=True)
    weights = lax.slice_in_dim(back_weights, 0, piece.shape[0], axis=1)
    part_re = jnp.einsum(
        "k,kzy->zy", weights[0], piece[:, 0], precision=lax.Precision.HIGHEST
    ) - jnp.einsum("k,kzy->zy", weights[1], piece[:, 1], precision=lax.Precision.HIGHEST)
    part_im = jnp.einsum(
        "k,kzy->zy", weights[0], piece[:, 1], precision=lax.Precision.HIGHEST
    ) + jnp.einsum("k,kzy->zy", weights[1], piece[:, 0], precision=lax.Precision.HIGHEST)
    next_first = jnp.zeros_like(nu_here) + jnp.stack([part_re, part_im])
    first_here = cmul(mu_here, next_first) + nu_here
    edge_prev = cmul(alpha_here, first_here) + beta_prev
    from_left = cmul(g_vec[:, :, None, None], edge_prev[:, None])
    from_right = cmul(h_vec[:, :, None, None], next_first[:, None])
    return local + from_left + from_right - turned


def solution(mesh):
    return jax.shard_map(
        shards,
        mesh=mesh,
        in_specs=(P(None, "gx", None, "gy"), P("gx", None, "gy")),
        out_specs=P(None, "gx", None, "gy"),
        check_vma=False,
    )
```

profile of v0, /device:TPU:0, one launch (start us, length us, event | category | flops | bytes accessed | tf_op | source)
XLA Modules:
  0.0 309.6 jit_solution(17856614827695865240)
XLA Ops:
  0.0 3.6 %fusion.18 = (f32[32,16,256]{2,1,0:T(8,128)S(1)}, f32[32,16,256]{2,1,0:T(8,128)S(1)}) fusion(f32[2,32,16,256]{3,2,1,0:T(8,128)} %param.11, f32[32,16,256]{2,1,0:T(8,128)} %param.12), kind=kLoop, calls=%fused_computation.56 | loop fusion | flops 1441792 | bytes 2621440 | tf_op jit(solution)/shard_map/add | solution.py:90
  3.9 1.3 collective-permute-start
  5.2 3.8 %collective-permute-start.1 = (f32[2,32,16,1]{3,2,1,0:T(8,128)S(1)}, f32[2,32,16,1]{3,2,1,0:T(8,128)}, u32[]{:S(2)}, u32[]{:S(2)}) collective-permute-start(f32[2,32,16,1]{3,2,1,0:T(8,128)S(1)} %get-tuple-element.456), channel_id=1, source_target_pairs={{0,1},{1,2},{2,3},{4,5},{5,6},{6,7},{8,9},{9,10},{10,11},{12,13},{... | collective-permute-start | bytes 12296 | tf_op jit(solution)/shard_map/ppermute | solution.py:17
  9.7 162.3 %while.56 = (s32[]{:T(128)}, f32[2]{0:T(128)S(1)}, f32[8,2]{1,0:T(8,128)S(1)}, f32[8,2]{1,0:T(8,128)S(1)}, f32[8,2]{1,0:T(8,128)S(1)}, /*index=5*/f32[8,2]{1,0:T...) while((s32[]{:T(128)}, f32[2]{0:T(128)S(1)}, ...), condition=%wide.region_1.2_spmd.clone.clone, body=%wide.region_0.1_spmd.clone.clone.sunk | while | flops 63 | bytes 928 | solution.py:122
  10.3 0.7 fusion.85
  30.6 0.7 fusion.85
  50.9 0.7 fusion.85
  71.2 0.7 fusion.85
  91.5 0.7 fusion.85
  111.7 0.7 fusion.85
  132.0 0.7 fusion.85
  152.3 0.7 fusion.85
  172.0 0.6 fusion.66
  173.8 26.4 %while.55 = (s32[]{:T(128)}, f32[2,8]{1,0:T(2,128)S(1)}, f32[8,2,8]{2,1,0:T(2,128)S(1)}, f32[8,2]{1,0:T(8,128)S(1)}, s32[8]{0:T(128)S(1)}, /*index=5*/s32[]{:T(128)}, s32[]{:T(128)}) while((s32[]{:T(128)}, f32[2,8]{1,0:T(2,128)S(1)}, f32[8,2,8]{2,1,0:T(2,128)S(1)}, f32[8,2]{1,0:T(8,128)S(1)}, s32[8]{0:T(128)S(1)}, ...), condition=%wide.region_5.6_spmd.clone.clone, body=%wide.region_4.5_spmd.clone.clone.sunk | while | flops 123 | bytes 3535 | solution.py:137
  173.8 0.7 dynamic_slice.70
  174.5 0.7 compare_bitcast_fusion.5
  175.8 1.3 multiply_subtract_fusion.10
  177.1 0.7 dynamic_slice.70
  177.8 0.7 compare_bitcast_fusion.5
  179.1 1.3 multiply_subtract_fusion.10
  180.4 0.7 dynamic_slice.70
  181.1 0.7 compare_bitcast_fusion.5
  182.4 1.3 multiply_subtract_fusion.10
  183.7 0.7 dynamic_slice.70
  184.4 0.7 compare_bitcast_fusion.5
  185.7 1.3 multiply_subtract_fusion.10
  187.0 0.7 dynamic_slice.70
  187.7 0.7 compare_bitcast_fusion.5
  189.0 1.3 multiply_subtract_fusion.10
  190.4 0.7 dynamic_slice.70
  191.0 0.7 compare_bitcast_fusion.5
  192.3 1.3 multiply_subtract_fusion.10
  193.7 0.7 dynamic_slice.70
  194.3 0.7 compare_bitcast_fusion.5
  195.7 1.3 multiply_subtract_fusion.10
  197.0 0.7 dynamic_slice.70
  197.6 0.7 compare_bitcast_fusion.5
  199.0 1.3 multiply_subtract_fusion.10
  200.3 26.6 %while.54 = (s32[]{:T(128)}, f32[2,8]{1,0:T(2,128)S(1)}, f32[8,2,8]{2,1,0:T(2,128)S(1)}, f32[8,2]{1,0:T(8,128)S(1)}, s32[8]{0:T(128)S(1)}, /*index=5*/s32[]{:T(128)}, s32[]{:T(128)}, s32[]{:T(128)}) while((s32[]{:T(128)}, f32[2,8]{1,0:T(2,128)S(1)}, f32[8,2,8]{2,1,0:T(2,128)S(1)}, f32[8,2]{1,0:T(8,128)S(1)}, ...), condition=%wide.region_3.4_spmd.clone.clone, body=%wide.region_2.3_spmd.clone.clone.sunk | while | flops 124 | bytes 3555 | solution.py:157
  201.6 0.7 fusion.80
  202.3 1.3 multiply_subtract_fusion.9
  204.9 0.7 fusion.80
  205.6 1.3 multiply_subtract_fusion.9
  208.2 0.7 fusion.80
  208.9 1.3 multiply_subtract_fusion.9
  211.6 0.7 fusion.80
  212.2 1.3 multiply_subtract_fusion.9
  214.9 0.7 fusion.80
  215.6 1.3 multiply_subtract_fusion.9
  218.2 0.7 fusion.80
  218.9 1.3 multiply_subtract_fusion.9
  221.5 0.7 fusion.80
  222.2 1.3 multiply_subtract_fusion.9
  224.8 0.7 fusion.80
  225.5 1.3 multiply_subtract_fusion.9
  232.1 1.9 fusion.5
  235.1 1.0 fusion.68
  236.5 32.7 %all_gather.6 = f32[8,2,16,256]{3,2,1,0:T(8,128)S(1)} all-gather(f32[1,2,16,256]{3,2,1,0:T(8,128)S(1)} %fusion.37), channel_id=1, replica_groups=mesh['gx'=8,'gy'=4] {'gx'}, dimensions={0}, use_global_device_ids=true | all-gather | bytes 294912 | tf_op jit(solution)/shard_map/all_gather | solution.py:139
  270.6 1.3 multiply_subtract_fusion.5
  271.9 30.7 %all-gather = f32[16,16,256]{2,1,0:T(8,128)S(1)} all-gather(f32[2,16,256]{2,1,0:T(8,128)S(1)} %pad_maximum_fusion.6), channel_id=2, replica_groups=mesh['gx'=8,'gy'=4] {'gx'}, dimensions={0}, use_global_device_ids=true | all-gather | bytes 294912 | tf_op jit(solution)/shard_map/all_gather | solution.py:161
  303.9 1.2 subtract_bitcast_fusion
  305.1 1.2 add_bitcast_fusion
  306.4 1.4 multiply_subtract_fusion.4
  308.2 1.5 fusion.9
  (237 shorter events, 34.9 us)
Async XLA Ops:
  3.9 228.2 %collective-permute-start = (f32[2,32,16,1]{3,2,1,0:T(8,128)S(1)}, f32[2,32,16,1]{3,2,1,0:T(8,128)}, u32[]{:S(2)}, u32[]{:S(2)}) collective-permute-start(f32[2,32,16,1]{3,2,1,0:T(8,128)S(1)} %get-tuple-element.455), channel_id=1, source_target_pairs={{1,0},{2,1},{3,2},{5,4},{6,5},{7,6},{9,8},{10,9},{11,10},{13,12},{... | collective-permute-start | bytes 12296 | tf_op jit(solution)/shard_map/ppermute | solution.py:18
  5.2 226.9 %collective-permute-start.1 = (f32[2,32,16,1]{3,2,1,0:T(8,128)S(1)}, f32[2,32,16,1]{3,2,1,0:T(8,128)}, u32[]{:S(2)}, u32[]{:S(2)}) collective-permute-start(f32[2,32,16,1]{3,2,1,0:T(8,128)S(1)} %get-tuple-element.456), channel_id=1, source_target_pairs={{0,1},{1,2},{2,3},{4,5},{5,6},{6,7},{8,9},{9,10},{10,11},{12,13},{... | collective-permute-start | bytes 12296 | tf_op jit(solution)/shard_map/ppermute | solution.py:17
  9.0 0.7 copy-start
  9.0 0.7 copy-start.1
  9.0 0.7 copy-start.3
  234.4 0.8 copy-start.2
  270.6 37.2 %copy-start.6 = (f32[32]{0:T(128)S(1)}, f32[32]{0:T(128)}, u32[]{:S(2)}) copy-start(f32[32]{0:T(128)} %constant.154) | copy-start | bytes 388
  270.6 37.2 %copy-start.7 = (f32[32]{0:T(128)S(1)}, f32[32]{0:T(128)}, u32[]{:S(2)}) copy-start(f32[32]{0:T(128)} %constant.152) | copy-start | bytes 388
  302.9 5.0 %copy-start.4 = (f32[32]{0:T(128)S(1)}, f32[32]{0:T(128)}, u32[]{:S(2)}) copy-start(f32[32]{0:T(128)} %constant.150) | copy-start | bytes 388
  303.0 5.0 %copy-start.5 = (f32[32]{0:T(128)S(1)}, f32[32]{0:T(128)}, u32[]{:S(2)}) copy-start(f32[32]{0:T(128)} %constant.131) | copy-start | bytes 388
where the time goes:
time: 313 us; the launch traced here: 310 us
  loops' own time  144 us (46%)
  blocking collectives  63.5 us (20%)
  other arithmetic  47.9 us (15%)
  local copies, waits for them, and re-layouts  39.6 us (13%)
  between operations  5.62 us (2%)
  starting transfers between devices  5.13 us (2%)
  matrix products  3.47 us (1%)
    another operation x1, loops' own time, shards(): lax.scan(advance, jnp.zeros((2,), jnp.float32), None, length=count)  144 us
    all_gather x1, blocking collectives, shards(): piece = lax.all_gather(fwd_term[None], 'gx', axis=0, tiled=True)  32.7 us
    all_gather x1, blocking collectives, shards(): piece = lax.all_gather(nu_here[None], 'gx', axis=0, tiled=True)  30.7 us
    sub x21, other arithmetic, cmul(): left[0] * right[0] - left[1] * right[1]  23.7 us
    slice x18, local copies, waits for them, and re-layouts, cmul(): left[0] * right[0] - left[1] * right[1]  11.3 us
    dynamic_slice x32, local copies, waits for them, and re-layouts, shards(): lax.scan(fwd_row, jnp.zeros((2, count), jnp.float32), (c_vals, positions))  10.4 us
  transfers between devices with their start and end apart: 2, of which 0 were waited for; matrix products, arithmetic and copies ran while one was open for 23% of the time, Pallas kernels for 0%

commit v1 on v0

--- a/solution.py
+++ b/solution.py
@@ -1,3 +1,4 @@
+import functools
 import jax
 import jax.numpy as jnp
 import numpy as np
@@ -5,6 +6,17 @@
 from jax.sharding import PartitionSpec as P
 
 RYZ = 2
+
+
+def work_the_vector(unit, a_name):
+    fresh = lax.axis_size(a_name)
+    all_rows = jnp.stack([unit] * fresh, 0)
+    arr_next = lax.all_to_all(all_rows, a_name, 0, 0)
+    finding = jnp.concatenate(arr_next, axis=0)
+    return finding
+
+
+match_chains = functools.partial(work_the_vector, a_name="gx")
 
 
 def with_halo(value, sides, width):
@@ -136,7 +148,7 @@
 
     unused, fwd_rows = lax.scan(fwd_row, jnp.zeros((2, count), jnp.float32), (c_vals, positions))
     fwd_weights = lax.dynamic_index_in_dim(fwd_rows, place, 0, keepdims=False)
-    piece = lax.all_gather(fwd_term[None], "gx", axis=0, tiled=True)
+    piece = match_chains(fwd_term[None])
     weights = lax.slice_in_dim(fwd_weights, 0, piece.shape[0], axis=1)
     part_re = jnp.einsum(
         "k,kzy->zy", weights[0], piece[:, 0], precision=lax.Precision.HIGHEST

time: 313 us -> 288 us (0.920)
  blocking collectives: 63.5 us -> 31.3 us
  starting transfers between devices: 5.13 us -> 12.4 us
    all_gather x1 -> x0, blocking collectives: 32.7 us -> none  [shards(): piece = lax.all_gather(fwd_term[None], 'gx', axis=0, tiled=True)]
    all_to_all x0 -> x1, starting transfers between devices: none -> 7.31 us  [work_the_vector(): arr_next = lax.all_to_all(all_rows, a_name, 0, 0)]
    sub x21 -> x20, other arithmetic: 23.7 us -> 22.6 us  [cmul(): left[0] * right[0] - left[1] * right[1]]
  transfers between devices with their start and end apart: 2 -> 3, of which waited for: 0 -> 0; matrix products, arithmetic and copies ran while one was open for 23% -> 25% of each run, Pallas kernels for 0% -> 0%
where the time goes in v1:
time: 288 us; the launch traced here: 285 us
  loops' own time  146 us (51%)
  other arithmetic  46.5 us (16%)
  local copies, waits for them, and re-layouts  40.1 us (14%)
  blocking collectives  31.3 us (11%)
  starting transfers between devices  12.4 us (4%)
  between operations  5.37 us (2%)
  matrix products  3.47 us (1%)
    another operation x1, loops' own time, shards(): lax.scan(advance, jnp.zeros((2,), jnp.float32), None, length=count)  145 us
    all_gather x1, blocking collectives, shards(): piece = lax.all_gather(nu_here[None], 'gx', axis=0, tiled=True)  31.3 us
    sub x20, other arithmetic, cmul(): left[0] * right[0] - left[1] * right[1]  22.6 us
    slice x18, local copies, waits for them, and re-layouts, cmul(): left[0] * right[0] - left[1] * right[1]  10.9 us
    dynamic_slice x32, local copies, waits for them, and re-layouts, shards(): lax.scan(fwd_row, jnp.zeros((2, count), jnp.float32), (c_vals, positions))  9.76 us
    all_to_all x1, starting transfers between devices, work_the_vector(): arr_next = lax.all_to_all(all_rows, a_name, 0, 0)  7.31 us
    slice x9, local copies, waits for them, and re-layouts, cmul(): left[1] * right[1]  5.8 us
  transfers between devices with their start and end apart: 3, of which 0 were waited for; matrix products, arithmetic and copies ran while one was open for 25% of the time, Pallas kernels for 0%

profile of v1, /device:TPU:0, one launch (start us, length us, event | category | flops | bytes accessed | tf_op | source)
XLA Modules:
  0.0 285.2 jit_solution(15327447686890287191)
XLA Ops:
  0.0 3.6 %fusion.18 = (f32[32,16,256]{2,1,0:T(8,128)S(1)}, f32[32,16,256]{2,1,0:T(8,128)S(1)}) fusion(f32[2,32,16,256]{3,2,1,0:T(8,128)} %param.11, f32[32,16,256]{2,1,0:T(8,128)} %param.12), kind=kLoop, calls=%fused_computation.56 | loop fusion | flops 1441792 | bytes 2621440 | tf_op jit(solution)/shard_map/add | solution.py:102
  3.9 1.3 collective-permute-start
  5.2 3.8 %collective-permute-start.1 = (f32[2,32,16,1]{3,2,1,0:T(8,128)S(1)}, f32[2,32,16,1]{3,2,1,0:T(8,128)}, u32[]{:S(2)}, u32[]{:S(2)}) collective-permute-start(f32[2,32,16,1]{3,2,1,0:T(8,128)S(1)} %get-tuple-element.456), channel_id=1, source_target_pairs={{0,1},{1,2},{2,3},{4,5},{5,6},{6,7},{8,9},{9,10},{10,11},{12,13},{... | collective-permute-start | bytes 12296 | tf_op jit(solution)/shard_map/ppermute | solution.py:29
  9.7 164.8 %while.56 = (s32[]{:T(128)}, f32[2]{0:T(128)S(1)}, f32[8,2]{1,0:T(8,128)S(1)}, f32[8,2]{1,0:T(8,128)S(1)}, f32[8,2]{1,0:T(8,128)S(1)}, /*index=5*/f32[8,2]{1,0:T...) while((s32[]{:T(128)}, f32[2]{0:T(128)S(1)}, ...), condition=%wide.region_1.2_spmd.clone.clone, body=%wide.region_0.1_spmd.clone.clone.sunk | while | flops 63 | bytes 928 | solution.py:134
  9.7 0.7 fusion.84
  10.3 0.7 fusion.85
  30.3 0.7 fusion.84
  30.9 0.7 fusion.85
  50.9 0.7 fusion.84
  51.6 0.7 fusion.85
  71.5 0.7 fusion.84
  72.2 0.7 fusion.85
  92.1 0.7 fusion.84
  92.8 0.7 fusion.85
  112.7 0.7 fusion.84
  113.4 0.7 fusion.85
  133.3 0.7 fusion.84
  134.0 0.7 fusion.85
  153.9 0.7 fusion.84
  154.6 0.7 fusion.85
  175.1 25.5 %while.54 = (s32[]{:T(128)}, f32[2,8]{1,0:T(2,128)S(1)}, f32[8,2,8]{2,1,0:T(2,128)S(1)}, f32[8,2]{1,0:T(8,128)S(1)}, s32[8]{0:T(128)S(1)}, /*index=5*/s32[]{:T(128)}, s32[]{:T(128)}, s32[]{:T(128)}) while((s32[]{:T(128)}, f32[2,8]{1,0:T(2,128)S(1)}, f32[8,2,8]{2,1,0:T(2,128)S(1)}, f32[8,2]{1,0:T(8,128)S(1)}, ...), condition=%wide.region_3.4_spmd.clone.clone, body=%wide.region_2.3_spmd.clone.clone.sunk | while | flops 124 | bytes 3555 | solution.py:169
  175.7 0.6 compare_bitcast_fusion.4
  177.0 1.3 multiply_subtract_fusion.8
  178.9 0.6 compare_bitcast_fusion.4
  180.2 1.3 multiply_subtract_fusion.8
  182.1 0.6 compare_bitcast_fusion.4
  183.4 1.3 multiply_subtract_fusion.8
  185.3 0.6 compare_bitcast_fusion.4
  186.6 1.3 multiply_subtract_fusion.8
  188.5 0.6 compare_bitcast_fusion.4
  189.8 1.3 multiply_subtract_fusion.8
  191.7 0.6 compare_bitcast_fusion.4
  193.0 1.3 multiply_subtract_fusion.8
  194.9 0.6 compare_bitcast_fusion.4
  196.2 1.3 multiply_subtract_fusion.8
  198.0 0.6 compare_bitcast_fusion.4
  199.3 1.3 multiply_subtract_fusion.8
  206.2 1.9 fusion.5
  209.2 1.0 fusion.68
  210.6 0.7 stack.197
  211.3 7.3 %all-to-all-start = ((f32[8,1,2,16,256]{4,3,2,1,0:T(8,128)}), f32[8,1,2,16,256]{4,3,2,1,0:T(8,128)S(1)}, u32[]{:S(2)}, u32[]{:S(2)}) async-start(f32[8,1,2,16,256]{4,3,2,1,0:T(8,128)} %stack.197), calls=%async_computation | async-start | bytes 524288 | tf_op jit(solution)/shard_map/all_to_all | solution.py:14
  218.7 25.0 %while.55 = (s32[]{:T(128)}, f32[2,8]{1,0:T(2,128)S(1)}, f32[8,2,8]{2,1,0:T(2,128)S(1)}, f32[8,2]{1,0:T(8,128)S(1)}, s32[8]{0:T(128)S(1)}, /*index=5*/s32[]{:T(128)}, s32[]{:T(128)}) while((s32[]{:T(128)}, f32[2,8]{1,0:T(2,128)S(1)}, f32[8,2,8]{2,1,0:T(2,128)S(1)}, f32[8,2]{1,0:T(8,128)S(1)}, s32[8]{0:T(128)S(1)}, ...), condition=%wide.region_5.6_spmd.clone.clone, body=%wide.region_4.5_spmd.clone.clone.sunk | while | flops 123 | bytes 3535 | solution.py:149
  219.3 0.6 compare_bitcast_fusion.5
  220.6 1.2 multiply_subtract_fusion.9
  222.4 0.6 compare_bitcast_fusion.5
  223.7 1.2 multiply_subtract_fusion.9
  225.6 0.6 compare_bitcast_fusion.5
  226.8 1.2 multiply_subtract_fusion.9
  228.7 0.6 compare_bitcast_fusion.5
  229.9 1.2 multiply_subtract_fusion.9
  231.8 0.6 compare_bitcast_fusion.5
  233.1 1.2 multiply_subtract_fusion.9
  234.9 0.6 compare_bitcast_fusion.5
  236.2 1.2 multiply_subtract_fusion.9
  238.1 0.6 compare_bitcast_fusion.5
  239.3 1.2 multiply_subtract_fusion.9
  241.2 0.6 compare_bitcast_fusion.5
  242.5 1.2 multiply_subtract_fusion.9
  245.7 1.3 multiply_subtract_fusion.5
  247.0 31.3 %all-gather = f32[16,16,256]{2,1,0:T(8,128)S(1)} all-gather(f32[2,16,256]{2,1,0:T(8,128)S(1)} %pad_maximum_fusion.6), channel_id=2, replica_groups=mesh['gx'=8,'gy'=4] {'gx'}, dimensions={0}, use_global_device_ids=true | all-gather | bytes 294912 | tf_op jit(solution)/shard_map/all_gather | solution.py:173
  279.6 1.2 subtract_bitcast_fusion
  280.8 1.2 add_bitcast_fusion
  282.0 1.2 multiply_subtract_fusion.4
  283.7 1.5 fusion.9
  (238 shorter events, 35.7 us)
Async XLA Ops:
  3.9 202.3 %collective-permute-start = (f32[2,32,16,1]{3,2,1,0:T(8,128)S(1)}, f32[2,32,16,1]{3,2,1,0:T(8,128)}, u32[]{:S(2)}, u32[]{:S(2)}) collective-permute-start(f32[2,32,16,1]{3,2,1,0:T(8,128)S(1)} %get-tuple-element.455), channel_id=1, source_target_pairs={{1,0},{2,1},{3,2},{5,4},{6,5},{7,6},{9,8},{10,9},{11,10},{13,12},{... | collective-permute-start | bytes 12296 | tf_op jit(solution)/shard_map/ppermute | solution.py:30
  5.2 201.0 %collective-permute-start.1 = (f32[2,32,16,1]{3,2,1,0:T(8,128)S(1)}, f32[2,32,16,1]{3,2,1,0:T(8,128)}, u32[]{:S(2)}, u32[]{:S(2)}) collective-permute-start(f32[2,32,16,1]{3,2,1,0:T(8,128)S(1)} %get-tuple-element.456), channel_id=1, source_target_pairs={{0,1},{1,2},{2,3},{4,5},{5,6},{6,7},{8,9},{9,10},{10,11},{12,13},{... | collective-permute-start | bytes 12296 | tf_op jit(solution)/shard_map/ppermute | solution.py:29
  9.0 0.7 copy-start
  9.0 0.7 copy-start.1
  9.0 0.7 copy-start.3
  208.5 0.8 copy-start.2
  211.3 33.0 %all-to-all-start = ((f32[8,1,2,16,256]{4,3,2,1,0:T(8,128)}), f32[8,1,2,16,256]{4,3,2,1,0:T(8,128)S(1)}, u32[]{:S(2)}, u32[]{:S(2)}) async-start(f32[8,1,2,16,256]{4,3,2,1,0:T(8,128)} %stack.197), calls=%async_computation | async-start | bytes 524288 | tf_op jit(solution)/shard_map/all_to_all | solution.py:14
  245.6 37.6 %copy-start.6 = (f32[32]{0:T(128)S(1)}, f32[32]{0:T(128)}, u32[]{:S(2)}) copy-start(f32[32]{0:T(128)} %constant.154) | copy-start | bytes 388
  245.7 37.6 %copy-start.7 = (f32[32]{0:T(128)S(1)}, f32[32]{0:T(128)}, u32[]{:S(2)}) copy-start(f32[32]{0:T(128)} %constant.152) | copy-start | bytes 388
  278.6 4.9 %copy-start.4 = (f32[32]{0:T(128)S(1)}, f32[32]{0:T(128)}, u32[]{:S(2)}) copy-start(f32[32]{0:T(128)} %constant.150) | copy-start | bytes 388
  278.6 4.9 %copy-start.5 = (f32[32]{0:T(128)S(1)}, f32[32]{0:T(128)}, u32[]{:S(2)}) copy-start(f32[32]{0:T(128)} %constant.131) | copy-start | bytes 388
